TPU v7x, 256 devices: a whole 4x4x8 slice. The times are simulated.
256 devices in a mesh: row: 4 (over z_lo, core), col: 64 (over y, x, z_hi).
Axes of the slice: x: 4, y: 4, z: 8 (z_hi: 4, z_lo: 2; z = z_hi * 2 + z_lo), core: 2. Of those that a mesh axis runs over, the one named last changes fastest.
Arguments:
- matrix_t: bfloat16 [30720, 30720], P('col', 'row')
- fibers: float32 [3, 131072], P(None, 'col'), may hold values from -0.7 to 0.7, as said below
- forces: float32 [3, 131072], P(None, 'col'), may hold values from -0.375 to 0.375
- nodes: float32 [3, 10240], P(None, 'row'), may hold values from -1 to 1, as said below
- node_order: int32 [10240], replicated, may hold values from 0 to 10239, each once
Outputs:
- velocity: float32 [30720], P(('row', 'col'))
- density: float32 [30720], P(('row', 'col'))
Inputs may be any that keep to these rules, and one draw needn't show every extreme that they name: node_order holds every number below 10240 once. `nodes`: every node lies on the unit sphere about the anchor. `fibers`: every fiber point lies within distance 0.7 of the anchor.
All inputs are finite; a program needn't handle non-finite values.
Results may differ from a plain program's by a relative error of at most 0.00067.
Values may be sent and summed in bfloat16 or wider, within the bound.
A program may use at most 64 MiB of HBM per device.

v0:
```python
import math

import jax
import jax.numpy as jnp
from jax import lax
from jax.sharding import PartitionSpec as P

inv_eight_pi = 1.0 / (8.0 * math.pi)
tiny_eps = 1e-06


def stokeslet_sum(targets, sources, strengths):
    count_src = sources.shape[1]
    width_blk = math.gcd(count_src, 256)

    def advance(turn_index, running):
        source = lax.dynamic_slice_in_dim(sources, turn_index * width_blk, width_blk, 1)
        force_block = lax.dynamic_slice_in_dim(strengths, turn_index * width_blk, width_blk, 1)
        offset = targets[:, None, :] - source[:, :, None]
        inverse = 1.0 / jnp.sqrt(jnp.sum(offset * offset, axis=0))
        projected = jnp.sum(offset * force_block[:, :, None], axis=0) * (
            inverse * inverse * inverse
        )
        return running + jnp.sum(
            force_block[:, :, None] * inverse[None] + offset * projected[None], axis=1
        )

    running = lax.fori_loop(
        0, count_src // width_blk, advance, jnp.zeros(targets.shape, jnp.float32)
    )
    return running * inv_eight_pi


def givens_solve(initial_norm, entry_11, entry_21, entry_12, entry_22, entry_32):
    radius_one = jnp.sqrt(entry_11 * entry_11 + entry_21 * entry_21)
    cosine_one = entry_11 / radius_one
    sine_one = entry_21 / radius_one
    upper_12 = cosine_one * entry_12 + sine_one * entry_22
    lower_22 = cosine_one * entry_22 - sine_one * entry_12
    radius_two = jnp.sqrt(lower_22 * lower_22 + entry_32 * entry_32)
    weight_two = lower_22 / radius_two * (-sine_one * initial_norm) / radius_two
    weight_one = (cosine_one * initial_norm - upper_12 * weight_two) / radius_one
    return (weight_one, weight_two)


def shards(matrix_t, fibers, forces, nodes, node_order):
    width_cols = matrix_t.shape[0]
    block_rows = matrix_t.shape[1]
    piece_rows = block_rows // lax.axis_size("col")
    row_place = lax.axis_index("row")
    col_place = lax.axis_index("col")
    all_nodes = lax.all_gather(nodes, "row", axis=1, tiled=True)
    node_count = block_rows // 3
    my_order = lax.dynamic_slice_in_dim(node_order, row_place * node_count, node_count)
    targets = jnp.take(all_nodes, my_order, axis=1)

    def gather_whole(rounded):
        return lax.all_gather(rounded, "row", axis=0, tiled=True)

    def column_operand(vector):
        rounded = vector.astype(jnp.bfloat16)
        whole = gather_whole(rounded)
        return lax.dynamic_slice_in_dim(whole, col_place * width_cols, width_cols)

    def sum_dots(stacked):
        return lax.psum(stacked, "row")

    def apply_operator(vector):
        column_part = column_operand(vector)
        product = jnp.dot(column_part, matrix_t, preferred_element_type=jnp.float32)
        return lax.psum(product, "col") + vector

    def to_piece(vector):
        return lax.dynamic_slice_in_dim(vector, col_place * piece_rows, piece_rows)

    velocity = lax.psum(stokeslet_sum(targets, fibers, forces).T.reshape(-1), "col")
    initial_norm = jnp.sqrt(sum_dots(jnp.stack([jnp.sum(velocity * velocity)]))[0] + tiny_eps)
    basis_one = velocity / initial_norm
    image_one = apply_operator(basis_one)
    entry_11 = sum_dots(jnp.stack([jnp.sum(basis_one * image_one)]))[0]
    rest_one = image_one - entry_11 * basis_one
    entry_21 = jnp.sqrt(sum_dots(jnp.stack([jnp.sum(rest_one * rest_one)]))[0] + tiny_eps)
    basis_two = rest_one / entry_21
    image_two = apply_operator(basis_two)
    entry_12 = sum_dots(jnp.stack([jnp.sum(basis_one * image_two)]))[0]
    partial_two = image_two - entry_12 * basis_one
    entry_22 = sum_dots(jnp.stack([jnp.sum(basis_two * partial_two)]))[0]
    rest_two = partial_two - entry_22 * basis_two
    entry_32 = jnp.sqrt(sum_dots(jnp.stack([jnp.sum(rest_two * rest_two)]))[0] + tiny_eps)
    weight_one, weight_two = givens_solve(
        initial_norm, entry_11, entry_21, entry_12, entry_22, entry_32
    )
    density = weight_one * basis_one + weight_two * basis_two
    return (to_piece(velocity), to_piece(density))


def solution(mesh):
    return jax.shard_map(
        shards,
        mesh=mesh,
        in_specs=(P("col", "row"), P(None, "col"), P(None, "col"), P(None, "row"), P()),
        out_specs=(P(("row", "col")), P(("row", "col"))),
        check_vma=False,
    )
```

profile of v0, /device:TPU:32, one launch (start us, length us, event | category | flops | bytes accessed | tf_op | source)
XLA Modules:
  0.0 1286.1 jit_solution(4615934349465660564)
XLA Ops:
  2.7 33.6 %all_gather.9 = f32[3,10240]{0,1:T(8,128)} all-gather(f32[3,2560]{0,1:T(8,128)S(1)} %copy.15), channel_id=1, replica_groups=mesh['row'=4,'col'=64] {'row'}, dimensions={1}, use_global_device_ids=true | all-gather | bytes 153600 | tf_op jit(solution)/shard_map/all_gather | solution.py:52
  36.3 6.6 gather_fusion
  44.7 46.0 %while.14 = (s32[]{:T(128)}, f32[3,2560]{1,0:T(4,128)S(1)}, f32[3,2048]{1,0:T(4,128)}, f32[3,2560]{1,0:T(4,128)S(1)}, f32[3,2048]{1,0:T(4,128)}, /*index=5*/s32[]{:T(128)}, s32[]{:T(128)}, s32[]{:T(128)}, s32[]{:T(128)}) while((s32[]{:T(128)}, f32[3,2560]{1,0:T(4,128)S(1)}, f32[3,2048]{1,0:T(4,128)}, f32[3,2560]{1,0:T(4,128)S(1)}, ...), condition=%wide.region_4.5_spmd.clone, body=%wide.region_0.4_spmd.clone.sunk | while | flops 20323844 | bytes 21180568 | solution.py:28
  45.4 2.1 fusion.16
  48.3 2.1 fusion.18
  51.2 2.1 fusion.16
  54.0 2.1 fusion.18
  56.9 2.1 fusion.16
  59.8 2.1 fusion.18
  62.7 2.1 fusion.16
  65.5 2.1 fusion.18
  68.4 2.1 fusion.16
  71.3 2.1 fusion.18
  74.2 2.1 fusion.16
  77.0 2.1 fusion.18
  79.9 2.1 fusion.16
  82.8 2.1 fusion.18
  85.7 2.1 fusion.16
  88.5 2.1 fusion.18
  92.0 379.5 %psum.63 = f32[7680]{0:T(1024)S(1)} all-reduce(f32[7680]{0:T(1024)S(1)} %reshape.41), channel_id=1, replica_groups=mesh['row'=4,'col'=64] {'col'}, use_global_device_ids=true, to_apply=%region_5.6 | all-reduce | flops 7680 | bytes 61440 | tf_op jit(solution)/shard_map/psum | solution.py:76
  472.1 6.3 psum.64
  479.1 5.4 all-gather
  485.0 4.2 convolution_reduce_fusion.1
  489.2 370.2 %psum.65 = f32[7680]{0:T(1024)S(1)} all-reduce(f32[7680]{0:T(1024)S(1)} %convolution_reduce_fusion.1), channel_id=1, replica_groups=mesh['row'=4,'col'=64] {'col'}, use_global_device_ids=true, to_apply=%region_8.9 | all-reduce | flops 7680 | bytes 61440 | tf_op jit(solution)/shard_map/psum | solution.py:71
  860.0 6.3 psum.66
  867.6 7.0 psum.67
  877.3 5.4 all-gather.1
  883.1 4.2 convolution_reduce_fusion
  887.3 370.3 %psum.68 = f32[7680]{0:T(1024)S(1)} all-reduce(f32[7680]{0:T(1024)S(1)} %convolution_reduce_fusion), channel_id=1, replica_groups=mesh['row'=4,'col'=64] {'col'}, use_global_device_ids=true, to_apply=%region_13.14 | all-reduce | flops 7680 | bytes 61440 | tf_op jit(solution)/shard_map/psum | solution.py:71
  1258.2 6.4 psum.69
  1265.8 7.0 psum.70
  1276.6 6.3 psum.71
  (53 shorter events, 26.1 us)
where the time goes:
time: 1290 us
  blocking collectives  1200 us (93%)
  other arithmetic  50.4 us (4%)
  local copies, waits for them, and re-layouts  16.1 us (1%)
    psum x2, blocking collectives, apply_operator(): return lax.psum(product, 'col') + vector  740 us
    psum x1, blocking collectives, shards(): lax.psum(stokeslet_sum(targets, fibers, forces).T.reshape(-1), 'col')  380 us
    psum x6, blocking collectives, sum_dots(): return lax.psum(stacked, 'row')  39.1 us
    all_gather x1, blocking collectives, shards(): all_nodes = lax.all_gather(nodes, 'row', axis=1, tiled=True)  33.6 us

commit v1 on v0

v1 whole, which is shorter than its diff:
```python
import functools
import math

import jax
import jax.numpy as jnp
from jax import lax
from jax.experimental import pallas as pl
from jax.experimental.pallas import tpu as pltpu
from jax.sharding import PartitionSpec as P

MESH = pl.DeviceIdType.MESH
inv_eight_pi = 1.0 / (8.0 * math.pi)
tiny_eps = 1e-06
f32 = jnp.float32
bf16 = jnp.bfloat16

ROWS = 4
COLS = 64
TARGETS = 2560
SOURCES = 2048
BLOCK = 480
WIDTH = 7680
PLANE = 16


def pieces_of(value, count):
    found = []
    rest = value
    for _ in range(count):
        piece = rest.astype(bf16).astype(f32)
        found.append(piece)
        rest = rest - piece
    return found


def spread_nodes(nodes_ref, all_ref, send_sem, recv_sem, own_sem):
    row = lax.axis_index("row")
    barrier = pltpu.get_barrier_semaphore()
    for step in range(1, ROWS):
        other = lax.rem(row + step, ROWS)
        pl.semaphore_signal(
            barrier, inc=1, device_id={"row": other}, device_id_type=MESH
        )
    own = pltpu.make_async_copy(nodes_ref, all_ref.at[row], own_sem)
    own.start()
    pl.semaphore_wait(barrier, ROWS - 1)
    copies = []
    for step in range(1, ROWS):
        other = lax.rem(row + step, ROWS)
        copy = pltpu.make_async_remote_copy(
            src_ref=nodes_ref,
            dst_ref=all_ref.at[row],
            send_sem=send_sem.at[step],
            recv_sem=recv_sem.at[step],
            device_id={"row": other},
            device_id_type=MESH,
        )
        copy.start()
        copies.append(copy)
    own.wait()
    for copy in copies:
        copy.wait()


def stokes_kernel(
    nodes_ref,
    order_ref,
    fibers_ref,
    forces_ref,
    out_ref,
    index_ref,
    target_ref,
    feature_ref,
    column_ref,
    source_ref,
    pull_ref,
    weight_f,
    weight_s,
    sum_f,
    sum_s,
):
    row = lax.axis_index("row")
    index_ref[pl.ds(0, 20), :] = order_ref[row]
    index_ref[pl.ds(20, 4), :] = jnp.zeros((4, 128), jnp.int32)
    index = index_ref[...]
    high = index // 128
    low = index - high * 128
    found = tuple(jnp.zeros((24, 128), f32) for _ in range(3))

    def pick(part, found):
        found = list(found)
        for tile in range(20):
            hit = high == part * 20 + tile
            for k in range(3):
                line = nodes_ref[part, pl.ds(k, 1), pl.ds(tile * 128, 128)]
                line = jnp.broadcast_to(line, (24, 128))
                taken = jnp.take_along_axis(line, low, axis=1)
                found[k] = jnp.where(hit, taken, found[k])
        return tuple(found)

    found = lax.fori_loop(0, ROWS, pick, found)
    square = found[0] * found[0] + found[1] * found[1] + found[2] * found[2]
    lines = []
    for k in range(3):
        one, two, three = pieces_of(found[k], 3)
        lines += [one, two, one, three, one, two]
    lines += pieces_of(square, 3)
    feature_ref[...] = jnp.ones((32, TARGETS), f32)
    for slot, line in enumerate(lines):
        for tile in range(20):
            feature_ref[pl.ds(slot, 1), pl.ds(tile * 128, 128)] = line[tile : tile + 1]
    for k in range(3):
        for tile in range(20):
            target_ref[pl.ds(k, 1), pl.ds(tile * 128, 128)] = found[k][tile : tile + 1]
    column_ref[...] = feature_ref[...].astype(bf16)

    fibers = fibers_ref[...]
    forces = forces_ref[...]
    place = [fibers[k : k + 1] for k in range(3)]
    force = [forces[k : k + 1] for k in range(3)]
    source_square = place[0] * place[0] + place[1] * place[1] + place[2] * place[2]
    source_dot = place[0] * force[0] + place[1] * force[1] + place[2] * force[2]
    nought = jnp.zeros((1, SOURCES), f32)
    unit = jnp.ones((1, SOURCES), f32)

    def stack(parts, tail, total):
        rows = []
        for k in range(3):
            one, two, three = pieces_of(parts[k], 3)
            rows += [one, one, two, one, three, two]
        rows += tail + pieces_of(total, 3) + [nought] * 8
        return jnp.concatenate(rows, axis=0)

    near = stack([-2.0 * one for one in place], [unit] * 3, source_square)
    turn = stack(force, [nought] * 3, -source_dot)
    source_ref[...] = near.T.astype(bf16)
    pull_ref[...] = turn.T.astype(bf16)
    force_pieces = [pieces_of(one, 2) for one in force]
    place_pieces = [pieces_of(one, 2) for one in place]
    weight_f[...] = jnp.concatenate(
        [one[0] for one in force_pieces]
        + [one[1] for one in force_pieces]
        + [nought] * 10,
        axis=0,
    ).astype(bf16)
    weight_s[...] = jnp.concatenate(
        [one[0] for one in place_pieces]
        + [one[1] for one in place_pieces]
        + [unit]
        + [nought] * 9,
        axis=0,
    ).astype(bf16)
    sum_f[...] = jnp.zeros((16, TARGETS), f32)
    sum_s[...] = jnp.zeros((16, TARGETS), f32)
    wide = 512
    deep = 256

    def advance(turn_index, carry):
        at = pl.ds(pl.multiple_of((turn_index // (SOURCES // deep)) * wide, wide), wide)
        of = pl.ds(
            pl.multiple_of(lax.rem(turn_index, SOURCES // deep) * deep, deep), deep
        )
        columns = column_ref[:, at]
        square = jnp.dot(source_ref[of, :], columns, preferred_element_type=f32)
        along = jnp.dot(pull_ref[of, :], columns, preferred_element_type=f32)
        inverse = lax.rsqrt(square)
        projected = along * (inverse * inverse * inverse)
        inverse_high = inverse.astype(bf16)
        inverse_low = (inverse - inverse_high.astype(f32)).astype(bf16)
        projected_high = projected.astype(bf16)
        projected_low = (projected - projected_high.astype(f32)).astype(bf16)
        with_f = weight_f[:, of]
        with_s = weight_s[:, of]
        sum_f[:, at] += jnp.dot(
            with_f, inverse_high, preferred_element_type=f32
        ) + jnp.dot(with_f, inverse_low, preferred_element_type=f32)
        sum_s[:, at] += jnp.dot(
            with_s, projected_high, preferred_element_type=f32
        ) + jnp.dot(with_s, projected_low, preferred_element_type=f32)
        return carry

    lax.fori_loop(0, (TARGETS // wide) * (SOURCES // deep), advance, 0)
    total_f = sum_f[...]
    total_s = sum_s[...]
    for k in range(3):
        value = (
            total_f[k : k + 1]
            + total_f[3 + k : 4 + k]
            + target_ref[pl.ds(k, 1), :] * total_s[6:7]
            - (total_s[k : k + 1] + total_s[3 + k : 4 + k])
        ) * inv_eight_pi
        for tile in range(20):
            out_ref[tile * 3 + k] = value[:, tile * 128 : tile * 128 + 128]


def total_of(value):
    return jnp.sum(value, axis=1, keepdims=True)


def krylov_kernel(
    part_ref,
    matrix_ref,
    velocity_ref,
    density_ref,
    held,
    image_one,
    image_two,
    recv_one,
    recv_two,
    recv_three,
    dots,
    recv_dots,
    piece,
    recv_piece,
    spread,
    load_sem,
    send_sems,
    recv_sems,
    dot_send,
    dot_recv,
    piece_send,
    piece_recv,
):
    row = lax.axis_index("row")
    col = lax.axis_index("col")
    level = col // PLANE
    inside = lax.rem(col, PLANE)
    load = pltpu.make_async_copy(matrix_ref, held, load_sem)
    load.start()
    piece_row = level
    piece_col = inside * 4 + row
    piece_own = jnp.logical_and(piece_row == row, piece_col == col)
    from_row = lax.rem(col, 4)
    from_col = row * PLANE + col // 4
    self_in = level == row

    barrier = pltpu.get_barrier_semaphore()

    def greet(step, carry):
        other = lax.rem(col + step, COLS)

        @pl.when(jnp.logical_not(jnp.logical_and(level == row, step == 0)))
        def _():
            pl.semaphore_signal(
                barrier, inc=1, device_id=(level, other), device_id_type=MESH
            )

        @pl.when(step > 0)
        def _():
            pl.semaphore_signal(
                barrier, inc=1, device_id=(row, other), device_id_type=MESH
            )

        return carry

    lax.fori_loop(0, COLS, greet, 0)

    @pl.when(jnp.logical_not(piece_own))
    def _():
        pl.semaphore_signal(
            barrier, inc=1, device_id=(from_row, from_col), device_id_type=MESH
        )

    lane_node = lax.broadcasted_iota(jnp.int32, (256, 512), 0)
    lane_entry = lax.broadcasted_iota(jnp.int32, (256, 512), 1)
    base = lane_entry - 3 * (lane_node - 32 * lax.rem(col, 4))
    for k in range(3):
        spread[k] = jnp.where(
            jnp.logical_and(base == k, lane_entry < BLOCK), 1.0, 0.0
        ).astype(bf16)

    peers = 2 * COLS - self_in.astype(jnp.int32) - piece_own.astype(jnp.int32)
    pl.semaphore_wait(barrier, peers)

    def send_blocks(stage, source, target, stride, scale, count):
        def one(step, carry):
            place = lax.rem(step + col, COLS)
            block = place // 4
            to_row = lax.rem(place, 4)
            to_col = row * PLANE + block
            window = source.at[pl.ds((stride * block) // 4 * scale, count)]
            is_self = jnp.logical_and(to_row == row, to_col == col)

            @pl.when(is_self)
            def _():
                pltpu.make_async_copy(
                    window, target.at[col], recv_sems.at[stage]
                ).start()

            @pl.when(jnp.logical_not(is_self))
            def _():
                pltpu.make_async_remote_copy(
                    src_ref=window,
                    dst_ref=target.at[col],
                    send_sem=send_sems.at[stage],
                    recv_sem=recv_sems.at[stage],
                    device_id=(to_row, to_col),
                    device_id_type=MESH,
                ).start()

            return carry

        lax.fori_loop(0, COLS, one, 0)

    def await_blocks(stage, target):
        pltpu.make_async_copy(target, target, recv_sems.at[stage]).wait()

    def await_sent(stage, target):
        @pl.when(self_in)
        def _():
            some = target.at[pl.ds(0, COLS - 1)]
            pltpu.make_async_copy(some, some, send_sems.at[stage]).wait()

        @pl.when(jnp.logical_not(self_in))
        def _():
            pltpu.make_async_copy(target, target, send_sems.at[stage]).wait()

    def added(target):
        def one(step, running):
            return running + target[step]

        return lax.fori_loop(1, COLS, one, target[0], unroll=9)

    def send_piece(which, vector):
        chosen = vector[:, 0:128]
        for quarter in range(1, 4):
            chosen = jnp.where(
                row == quarter, vector[:, 120 * quarter : 120 * quarter + 128], chosen
            )
        piece[which] = chosen

        @pl.when(piece_own)
        def _():
            pltpu.make_async_copy(
                piece.at[which], recv_piece.at[which], piece_recv.at[which]
            ).start()

        @pl.when(jnp.logical_not(piece_own))
        def _():
            pltpu.make_async_remote_copy(
                src_ref=piece.at[which],
                dst_ref=recv_piece.at[which],
                send_sem=piece_send.at[which],
                recv_sem=piece_recv.at[which],
                device_id=(piece_row, piece_col),
                device_id_type=MESH,
            ).start()

    def await_piece(which):
        pltpu.make_async_copy(
            recv_piece.at[which], recv_piece.at[which], piece_recv.at[which]
        ).wait()

        @pl.when(jnp.logical_not(piece_own))
        def _():
            pltpu.make_async_copy(
                recv_piece.at[which], recv_piece.at[which], piece_send.at[which]
            ).wait()

    lane = lax.broadcasted_iota(jnp.int32, (1, 128), 1)

    def send_dots(which, values):
        line = jnp.zeros((1, 128), f32)
        for slot, value in enumerate(values):
            line = jnp.where(lane == slot, value, line)
        dots[which] = line

        def one(step, carry):
            pltpu.make_async_remote_copy(
                src_ref=dots.at[which],
                dst_ref=recv_dots.at[which, step - 1],
                send_sem=dot_send.at[which],
                recv_sem=dot_recv.at[which],
                device_id=(row, lax.rem(col + step, COLS)),
                device_id_type=MESH,
            ).start()
            return carry

        lax.fori_loop(1, COLS, one, 0)

    def await_dots(which, count):
        whole = recv_dots.at[which]
        pltpu.make_async_copy(whole, whole, dot_recv.at[which]).wait()

        def one(step, running):
            return running + recv_dots[which, step]

        line = lax.fori_loop(0, COLS - 1, one, dots[which], unroll=9)
        return [total_of(jnp.where(lane == slot, line, 0.0)) for slot in range(count)]

    def await_dots_sent(which):
        whole = recv_dots.at[which]
        pltpu.make_async_copy(whole, whole, dot_send.at[which]).wait()

    which_row = lax.broadcasted_iota(jnp.int32, (16, 512), 0)

    def multiply(vector, image):
        high, low = pieces_of(vector, 2)
        left = jnp.where(which_row == 0, high, jnp.where(which_row == 1, low, 0.0))
        left = left.astype(bf16)[:, :BLOCK]

        for step in range(WIDTH // 512):
            got = jnp.dot(
                left, held[:, step * 512 : step * 512 + 512], preferred_element_type=f32
            )
            got = got[0:1] + got[1:2]
            for tile in range(4):
                image[step * 4 + tile] = got[:, tile * 128 : tile * 128 + 128]

    offset = lax.rem(96 * lax.rem(col, 4), 128)
    lane_wide = lax.broadcasted_iota(jnp.int32, (1, 512), 1)

    def aligned(total):
        line = jnp.concatenate([total[tile] for tile in range(5)], axis=1)
        chosen = line[:, 0:512]
        for shift in (32, 64, 96):
            chosen = jnp.where(offset == shift, line[:, shift : shift + 512], chosen)
        return jnp.where(lane_wide < BLOCK, chosen, 0.0)

    send_blocks(0, part_ref, recv_one, 5, 3, 6)
    image_one[WIDTH // 128] = jnp.zeros((1, 128), f32)
    image_two[WIDTH // 128] = jnp.zeros((1, 128), f32)
    await_blocks(0, recv_one)
    total = added(recv_one)
    which_small = lax.broadcasted_iota(jnp.int32, (16, 256), 0)
    first = jnp.zeros((16, 512), f32)
    for k in range(3):
        line = jnp.concatenate([total[k], total[3 + k]], axis=1)
        one, two, three = pieces_of(line, 3)
        left = jnp.where(
            which_small == 0,
            one,
            jnp.where(which_small == 1, two, jnp.where(which_small == 2, three, 0.0)),
        )
        first = first + jnp.dot(
            left.astype(bf16), spread[k], preferred_element_type=f32
        )
    vector = first[0:1] + first[1:2] + first[2:3]
    load.wait()
    multiply(vector, image_one)
    send_blocks(1, image_one, recv_two, 15, 1, 5)
    send_piece(0, vector)
    await_blocks(1, recv_two)
    image = aligned(added(recv_two))
    multiply(image, image_two)
    send_blocks(2, image_two, recv_three, 15, 1, 5)
    send_piece(1, image)
    send_dots(
        0, [total_of(vector * vector), total_of(vector * image), total_of(image * image)]
    )
    vv, vw, ww = await_dots(0, 3)
    norm_square = vv + tiny_eps
    initial_norm = jnp.sqrt(norm_square)
    scale_one = 1.0 / initial_norm
    entry_11 = (vv + vw) / norm_square
    slide = (vw - tiny_eps) / norm_square
    rest_square = (ww - 2.0 * slide * vw + slide * slide * vv) / norm_square
    entry_21 = jnp.sqrt(jnp.maximum(rest_square, 0.0) + tiny_eps)
    scale_two = scale_one / entry_21
    basis_one = vector * scale_one
    basis_two = (image - slide * vector) * scale_two
    await_blocks(2, recv_three)
    last = (aligned(added(recv_three)) - slide * image) * scale_two
    send_dots(
        1,
        [
            total_of(basis_one * basis_one),
            total_of(basis_one * basis_two),
            total_of(basis_two * basis_two),
            total_of(basis_one * last),
            total_of(basis_two * last),
            total_of(last * last),
        ],
    )
    await_piece(0)
    await_piece(1)
    velocity_piece = recv_piece[0]
    image_piece = recv_piece[1]
    velocity_ref[...] = velocity_piece[:, :120]
    aa, ab, bb, al, bl, ll = await_dots(1, 6)
    entry_12 = ab + al
    entry_22 = bb + bl - entry_12 * ab
    from_one = -entry_12
    from_two = 1.0 - entry_22
    rest_two = (
        ll
        + from_one * from_one * aa
        + from_two * from_two * bb
        + 2.0 * (from_one * from_two * ab + from_one * al + from_two * bl)
    )
    entry_32 = jnp.sqrt(jnp.maximum(rest_two, 0.0) + tiny_eps)
    radius_one = jnp.sqrt(entry_11 * entry_11 + entry_21 * entry_21)
    cosine_one = entry_11 / radius_one
    sine_one = entry_21 / radius_one
    upper_12 = cosine_one * entry_12 + sine_one * entry_22
    lower_22 = cosine_one * entry_22 - sine_one * entry_12
    radius_two = jnp.sqrt(lower_22 * lower_22 + entry_32 * entry_32)
    weight_two = lower_22 / radius_two * (-sine_one * initial_norm) / radius_two
    weight_one = (cosine_one * initial_norm - upper_12 * weight_two) / radius_one
    result = weight_one * (velocity_piece * scale_one) + weight_two * (
        (image_piece - slide * velocity_piece) * scale_two
    )
    density_ref[...] = result[:, :120]
    await_sent(0, recv_one)
    await_sent(1, recv_two)
    await_sent(2, recv_three)
    await_dots_sent(0)
    await_dots_sent(1)


def in_vmem(count):
    return [pl.BlockSpec(memory_space=pltpu.VMEM)] * count


def shards(matrix_t, fibers, forces, nodes, node_order):
    all_nodes = pl.pallas_call(
        spread_nodes,
        name="spread_nodes",
        out_shape=jax.ShapeDtypeStruct((ROWS, 3, TARGETS), f32),
        in_specs=in_vmem(1),
        out_specs=in_vmem(1)[0],
        scratch_shapes=[
            pltpu.SemaphoreType.DMA((ROWS,)),
            pltpu.SemaphoreType.DMA((ROWS,)),
            pltpu.SemaphoreType.DMA,
        ],
        compiler_params=pltpu.CompilerParams(collective_id=0, has_side_effects=True),
    )(nodes)
    part = pl.pallas_call(
        stokes_kernel,
        name="stokes",
        out_shape=jax.ShapeDtypeStruct((TARGETS * 3 // 128, 1, 128), f32),
        in_specs=in_vmem(4),
        out_specs=in_vmem(1)[0],
        scratch_shapes=[
            pltpu.VMEM((24, 128), jnp.int32),
            pltpu.VMEM((8, TARGETS), f32),
            pltpu.VMEM((32, TARGETS), f32),
            pltpu.VMEM((32, TARGETS), bf16),
            pltpu.VMEM((SOURCES, 32), bf16),
            pltpu.VMEM((SOURCES, 32), bf16),
            pltpu.VMEM((16, SOURCES), bf16),
            pltpu.VMEM((16, SOURCES), bf16),
            pltpu.VMEM((16, TARGETS), f32),
            pltpu.VMEM((16, TARGETS), f32),
        ],
    )(all_nodes, node_order.reshape(ROWS, 20, 128), fibers, forces)
    velocity, density = pl.pallas_call(
        krylov_kernel,
        name="krylov",
        out_shape=[jax.ShapeDtypeStruct((1, 120), f32)] * 2,
        in_specs=in_vmem(1) + [pl.BlockSpec(memory_space=pl.ANY)],
        out_specs=in_vmem(2),
        scratch_shapes=[
            pltpu.VMEM((BLOCK, WIDTH), bf16),
            pltpu.VMEM((WIDTH // 128 + 1, 1, 128), f32),
            pltpu.VMEM((WIDTH // 128 + 1, 1, 128), f32),
            pltpu.VMEM((COLS, 6, 1, 128), f32),
            pltpu.VMEM((COLS, 5, 1, 128), f32),
            pltpu.VMEM((COLS, 5, 1, 128), f32),
            pltpu.VMEM((2, 1, 128), f32),
            pltpu.VMEM((2, COLS - 1, 1, 128), f32),
            pltpu.VMEM((2, 1, 128), f32),
            pltpu.VMEM((2, 1, 128), f32),
            pltpu.VMEM((3, 256, 512), bf16),
            pltpu.SemaphoreType.DMA,
            pltpu.SemaphoreType.DMA((3,)),
            pltpu.SemaphoreType.DMA((3,)),
            pltpu.SemaphoreType.DMA((2,)),
            pltpu.SemaphoreType.DMA((2,)),
            pltpu.SemaphoreType.DMA((2,)),
            pltpu.SemaphoreType.DMA((2,)),
        ],
        compiler_params=pltpu.CompilerParams(collective_id=1, has_side_effects=True),
    )(part, matrix_t)
    return velocity.reshape(120), density.reshape(120)


def solution(mesh):
    return jax.shard_map(
        shards,
        mesh=mesh,
        in_specs=(P("col", "row"), P(None, "col"), P(None, "col"), P(None, "row"), P()),
        out_specs=(P(("row", "col")), P(("row", "col"))),
        check_vma=False,
    )
```

time: 1290 us -> 86.9 us (0.07)
  blocking collectives: 1200 us -> 0 us
  Pallas kernels: 0 us -> 81.8 us
  other arithmetic: 50.4 us -> 0 us
    psum x9 -> x0, blocking collectives: 1160 us -> none  [the longest x2 740 us: apply_operator(): return lax.psum(product, 'col') + vector]
    pallas_call x0 -> x3, Pallas kernels: none -> 81.8 us  [the longest x1 52 us: shards(): pl.pallas_call(krylov_kernel, name='krylov', out_shape=[jax.ShapeDtypeStr...]
    all_gather x3 -> x0, blocking collectives: 44.4 us -> none  [the longest x1 33.6 us: shards(): all_nodes = lax.all_gather(nodes, 'row', axis=1, tiled=True)]
    reduce_sum x22 -> x0, other arithmetic: 40 us -> none  [the longest x8 17 us: advance(): inverse = 1.0 / jnp.sqrt(jnp.sum(offset * offset, axis=0))]
where the time goes in v1:
time: 86.9 us; the launch traced here: 86.1 us
  Pallas kernels  81.8 us (94%)
  local copies, waits for them, and re-layouts  3.64 us (4%)
    pallas_call x1, Pallas kernels, shards(): pl.pallas_call(krylov_kernel, name='krylov', out_shape=[jax.ShapeDtypeStr...  52 us
    pallas_call x1, Pallas kernels, shards(): pl.pallas_call(stokes_kernel, name='stokes', out_shape=jax.ShapeDtypeStru...  23.8 us
    pallas_call x1, Pallas kernels, shards(): pl.pallas_call(spread_nodes, name='spread_nodes', out_shape=jax.ShapeDtyp...  5.96 us
    unnamed x2, local copies, waits for them, and re-layouts  2.25 us

profile of v1, /device:TPU:32, one launch (start us, length us, event | category | flops | bytes accessed | tf_op | source)
XLA Modules:
  0.0 86.1 jit_solution(16098681870999070674)
XLA Ops:
  0.6 1.4 %reshape.13.order_ref = s32[4,20,128]{2,1,0:T(8,128)} reshape(s32[10240]{0:T(1024)} %param.9) | data formatting | bytes 81920 | tf_op jit(solution)/shard_map/reshape | solution.py:547
  2.0 6.0 %spread_nodes.1.nodes_ref = f32[4,3,2560]{2,1,0:T(4,128)} custom-call(f32[3,2560]{1,0:T(4,128)} %nodes_ref.1), custom_call_target="tpu_custom_call" | custom-call | tf_op jit(solution)/shard_map/spread_nodes/pallas_call | solution.py:516
  8.0 23.8 %stokes.1.part_ref = f32[60,1,128]{2,1,0:T(1,128)} custom-call(f32[4,3,2560]{2,1,0:T(4,128)} %spread_nodes.1.nodes_ref, s32[4,20,128]{2,1,0:T(8,128)} %reshape.13.order_ref, f32[3,2048]{1,0:T(4,128)} %fibers_ref.1, f32[3,2048]{1,0:T(4,128)} %forces_ref.1), custom_call_target="tpu_custom_call" | custom-call | tf_op jit(solution)/shard_map/stokes/pallas_call | solution.py:529
  31.8 52.0 %krylov.1 = (f32[1,120]{1,0:T(1,128)}, f32[1,120]{1,0:T(1,128)}) custom-call(f32[60,1,128]{2,1,0:T(1,128)} %stokes.1.part_ref, bf16[480,7680]{1,0:T(8,128)(2,1)} %matrix_ref.1), custom_call_target="tpu_custom_call" | custom-call | tf_op jit(solution)/shard_map/krylov/pallas_call | solution.py:548
  83.9 1.1 %copy.9 = f32[120]{0:T(128)} copy(f32[120]{0:T(128)} %bitcast.3) | data formatting | bytes 960
  85.0 1.1 %copy.10 = f32[120]{0:T(128)} copy(f32[120]{0:T(128)} %bitcast.2) | data formatting | bytes 960

commit v2 on v1

--- a/solution.py
+++ b/solution.py
@@ -21,6 +21,11 @@
 BLOCK = 480
 WIDTH = 7680
 PLANE = 16
+WIDE = 256
+FAR = (2, 1, 3, 0)
+FAR_FIRST = [(z, x, r) for z in FAR for x in FAR for r in (1, 2, 3, 0)]
+PEERS_FIRST = [(z, x, y) for z in FAR for x in FAR for y in FAR if z or x or y]
+DEEP = 256
 
 
 def pieces_of(value, count):
@@ -62,7 +67,7 @@
         copy.wait()
 
 
-def stokes_kernel(
+def velocity_part(
     nodes_ref,
     order_ref,
     fibers_ref,
@@ -73,13 +78,33 @@
     feature_ref,
     column_ref,
     source_ref,
-    pull_ref,
-    weight_f,
-    weight_s,
-    sum_f,
-    sum_s,
+    weight_ref,
+    sum_ref,
 ):
     row = lax.axis_index("row")
+    fibers = fibers_ref[...]
+    forces = forces_ref[...]
+    place = [fibers[k : k + 1] for k in range(3)]
+    force = [forces[k : k + 1] for k in range(3)]
+    source_square = place[0] * place[0] + place[1] * place[1] + place[2] * place[2]
+    source_dot = place[0] * force[0] + place[1] * force[1] + place[2] * force[2]
+    nought = jnp.zeros((1, SOURCES), f32)
+    unit = jnp.ones((1, SOURCES), f32)
+    near = []
+    for k in range(3):
+        one, two, three = pieces_of(-2.0 * place[k], 3)
+        near += [one, one, two, one, three, two]
+    near += [unit] * 3 + pieces_of(source_square, 3) + [nought] * 8
+    source_ref[...] = jnp.concatenate(near, axis=0).T.astype(bf16)
+    moments = list(force)
+    for k in range(3):
+        moments += [place[k] * force[m] for m in range(3)]
+    moments += [source_dot] + [place[k] * source_dot for k in range(3)]
+    moments += [force[k] * source_square for k in range(3)]
+    moments = jnp.concatenate(moments + [nought] * 5, axis=0)
+    one, two = pieces_of(moments, 2)
+    weight_ref[...] = jnp.concatenate([one, two], axis=0).astype(bf16)
+
     index_ref[pl.ds(0, 20), :] = order_ref[row]
     index_ref[pl.ds(20, 4), :] = jnp.zeros((4, 128), jnp.int32)
     index = index_ref[...]
@@ -109,86 +134,47 @@
     for slot, line in enumerate(lines):
         for tile in range(20):
             feature_ref[pl.ds(slot, 1), pl.ds(tile * 128, 128)] = line[tile : tile + 1]
+    for slot, line in enumerate(list(found) + [square]):
+        for tile in range(20):
+            target_ref[pl.ds(slot, 1), pl.ds(tile * 128, 128)] = line[tile : tile + 1]
+    column_ref[...] = feature_ref[...].astype(bf16)
+
+    def across(turn, carry):
+        at = pl.ds(pl.multiple_of(turn * WIDE, WIDE), WIDE)
+        columns = column_ref[:, at]
+        running = jnp.zeros((48, WIDE), f32)
+        for chunk in range(SOURCES // DEEP):
+            of = pl.ds(chunk * DEEP, DEEP)
+            square = jnp.dot(source_ref[of, :], columns, preferred_element_type=f32)
+            inverse = lax.rsqrt(square)
+            cubed = inverse * inverse * inverse
+            cubed_high = cubed.astype(bf16)
+            cubed_low = (cubed - cubed_high.astype(f32)).astype(bf16)
+            weight = weight_ref[:, of]
+            running = (
+                running
+                + jnp.dot(weight, cubed_high, preferred_element_type=f32)
+                + jnp.dot(weight, cubed_low, preferred_element_type=f32)
+            )
+        sum_ref[:, at] = running[:24] + running[24:]
+        return carry
+
+    lax.fori_loop(0, TARGETS // WIDE, across, 0)
+    sums = sum_ref[...]
+    spots = target_ref[...]
+    spot = [spots[k : k + 1] for k in range(3)]
+    squared = spots[3:4]
+    plain = [sums[k : k + 1] for k in range(3)]
+    mixed = [[sums[3 + 3 * k + m : 4 + 3 * k + m] for m in range(3)] for k in range(3)]
+    along = (
+        spot[0] * plain[0] + spot[1] * plain[1] + spot[2] * plain[2] - sums[12:13]
+    )
     for k in range(3):
-        for tile in range(20):
-            target_ref[pl.ds(k, 1), pl.ds(tile * 128, 128)] = found[k][tile : tile + 1]
-    column_ref[...] = feature_ref[...].astype(bf16)
-
-    fibers = fibers_ref[...]
-    forces = forces_ref[...]
-    place = [fibers[k : k + 1] for k in range(3)]
-    force = [forces[k : k + 1] for k in range(3)]
-    source_square = place[0] * place[0] + place[1] * place[1] + place[2] * place[2]
-    source_dot = place[0] * force[0] + place[1] * force[1] + place[2] * force[2]
-    nought = jnp.zeros((1, SOURCES), f32)
-    unit = jnp.ones((1, SOURCES), f32)
-
-    def stack(parts, tail, total):
-        rows = []
-        for k in range(3):
-            one, two, three = pieces_of(parts[k], 3)
-            rows += [one, one, two, one, three, two]
-        rows += tail + pieces_of(total, 3) + [nought] * 8
-        return jnp.concatenate(rows, axis=0)
-
-    near = stack([-2.0 * one for one in place], [unit] * 3, source_square)
-    turn = stack(force, [nought] * 3, -source_dot)
-    source_ref[...] = near.T.astype(bf16)
-    pull_ref[...] = turn.T.astype(bf16)
-    force_pieces = [pieces_of(one, 2) for one in force]
-    place_pieces = [pieces_of(one, 2) for one in place]
-    weight_f[...] = jnp.concatenate(
-        [one[0] for one in force_pieces]
-        + [one[1] for one in force_pieces]
-        + [nought] * 10,
-        axis=0,
-    ).astype(bf16)
-    weight_s[...] = jnp.concatenate(
-        [one[0] for one in place_pieces]
-        + [one[1] for one in place_pieces]
-        + [unit]
-        + [nought] * 9,
-        axis=0,
-    ).astype(bf16)
-    sum_f[...] = jnp.zeros((16, TARGETS), f32)
-    sum_s[...] = jnp.zeros((16, TARGETS), f32)
-    wide = 512
-    deep = 256
-
-    def advance(turn_index, carry):
-        at = pl.ds(pl.multiple_of((turn_index // (SOURCES // deep)) * wide, wide), wide)
-        of = pl.ds(
-            pl.multiple_of(lax.rem(turn_index, SOURCES // deep) * deep, deep), deep
-        )
-        columns = column_ref[:, at]
-        square = jnp.dot(source_ref[of, :], columns, preferred_element_type=f32)
-        along = jnp.dot(pull_ref[of, :], columns, preferred_element_type=f32)
-        inverse = lax.rsqrt(square)
-        projected = along * (inverse * inverse * inverse)
-        inverse_high = inverse.astype(bf16)
-        inverse_low = (inverse - inverse_high.astype(f32)).astype(bf16)
-        projected_high = projected.astype(bf16)
-        projected_low = (projected - projected_high.astype(f32)).astype(bf16)
-        with_f = weight_f[:, of]
-        with_s = weight_s[:, of]
-        sum_f[:, at] += jnp.dot(
-            with_f, inverse_high, preferred_element_type=f32
-        ) + jnp.dot(with_f, inverse_low, preferred_element_type=f32)
-        sum_s[:, at] += jnp.dot(
-            with_s, projected_high, preferred_element_type=f32
-        ) + jnp.dot(with_s, projected_low, preferred_element_type=f32)
-        return carry
-
-    lax.fori_loop(0, (TARGETS // wide) * (SOURCES // deep), advance, 0)
-    total_f = sum_f[...]
-    total_s = sum_s[...]
-    for k in range(3):
-        value = (
-            total_f[k : k + 1]
-            + total_f[3 + k : 4 + k]
-            + target_ref[pl.ds(k, 1), :] * total_s[6:7]
-            - (total_s[k : k + 1] + total_s[3 + k : 4 + k])
-        ) * inv_eight_pi
+        value = squared * plain[k] + sums[16 + k : 17 + k] + spot[k] * along
+        value = value + sums[13 + k : 14 + k]
+        for m in range(3):
+            value = value - spot[m] * (2.0 * mixed[m][k] + mixed[k][m])
+        value = value * inv_eight_pi
         for tile in range(20):
             out_ref[tile * 3 + k] = value[:, tile * 128 : tile * 128 + 128]
 
@@ -198,10 +184,21 @@
 
 
 def krylov_kernel(
-    part_ref,
+    nodes_ref,
+    order_ref,
+    fibers_ref,
+    forces_ref,
     matrix_ref,
     velocity_ref,
     density_ref,
+    index_ref,
+    target_ref,
+    feature_ref,
+    column_ref,
+    source_ref,
+    weight_ref,
+    sum_ref,
+    part_ref,
     held,
     image_one,
     image_two,
@@ -269,38 +266,51 @@
             jnp.logical_and(base == k, lane_entry < BLOCK), 1.0, 0.0
         ).astype(bf16)
 
+    velocity_part(
+        nodes_ref,
+        order_ref,
+        fibers_ref,
+        forces_ref,
+        part_ref,
+        index_ref,
+        target_ref,
+        feature_ref,
+        column_ref,
+        source_ref,
+        weight_ref,
+        sum_ref,
+    )
     peers = 2 * COLS - self_in.astype(jnp.int32) - piece_own.astype(jnp.int32)
     pl.semaphore_wait(barrier, peers)
 
     def send_blocks(stage, source, target, stride, scale, count):
-        def one(step, carry):
-            place = lax.rem(step + col, COLS)
-            block = place // 4
-            to_row = lax.rem(place, 4)
+        for z_step, x_step, row_step in FAR_FIRST:
+            to_x = lax.rem(col // 4 + x_step, 4)
+            block = to_x * 4 + lax.rem(col + z_step, 4)
+            to_row = lax.rem(row + row_step, ROWS)
             to_col = row * PLANE + block
             window = source.at[pl.ds((stride * block) // 4 * scale, count)]
-            is_self = jnp.logical_and(to_row == row, to_col == col)
-
-            @pl.when(is_self)
-            def _():
-                pltpu.make_async_copy(
-                    window, target.at[col], recv_sems.at[stage]
-                ).start()
-
-            @pl.when(jnp.logical_not(is_self))
-            def _():
-                pltpu.make_async_remote_copy(
-                    src_ref=window,
-                    dst_ref=target.at[col],
-                    send_sem=send_sems.at[stage],
-                    recv_sem=recv_sems.at[stage],
-                    device_id=(to_row, to_col),
-                    device_id_type=MESH,
-                ).start()
-
-            return carry
-
-        lax.fori_loop(0, COLS, one, 0)
+            remote = pltpu.make_async_remote_copy(
+                src_ref=window,
+                dst_ref=target.at[col],
+                send_sem=send_sems.at[stage],
+                recv_sem=recv_sems.at[stage],
+                device_id=(to_row, to_col),
+                device_id_type=MESH,
+            )
+            if z_step or x_step or row_step:
+                remote.start()
+            else:
+
+                @pl.when(self_in)
+                def _():
+                    pltpu.make_async_copy(
+                        window, target.at[col], recv_sems.at[stage]
+                    ).start()
+
+                @pl.when(jnp.logical_not(self_in))
+                def _():
+                    remote.start()
 
     def await_blocks(stage, target):
         pltpu.make_async_copy(target, target, recv_sems.at[stage]).wait()
@@ -365,18 +375,18 @@
             line = jnp.where(lane == slot, value, line)
         dots[which] = line
 
-        def one(step, carry):
+        for slot, (z_step, x_step, y_step) in enumerate(PEERS_FIRST):
+            to_z = lax.rem(col + z_step, 4)
+            to_x = lax.rem(col // 4 + x_step, 4)
+            to_y = lax.rem(level + y_step, 4)
             pltpu.make_async_remote_copy(
                 src_ref=dots.at[which],
-                dst_ref=recv_dots.at[which, step - 1],
+                dst_ref=recv_dots.at[which, slot],
                 send_sem=dot_send.at[which],
                 recv_sem=dot_recv.at[which],
-                device_id=(row, lax.rem(col + step, COLS)),
+                device_id=(row, to_y * PLANE + to_x * 4 + to_z),
                 device_id_type=MESH,
             ).start()
-            return carry
-
-        lax.fori_loop(1, COLS, one, 0)
 
     def await_dots(which, count):
         whole = recv_dots.at[which]
@@ -526,32 +536,21 @@
         ],
         compiler_params=pltpu.CompilerParams(collective_id=0, has_side_effects=True),
     )(nodes)
-    part = pl.pallas_call(
-        stokes_kernel,
-        name="stokes",
-        out_shape=jax.ShapeDtypeStruct((TARGETS * 3 // 128, 1, 128), f32),
-        in_specs=in_vmem(4),
-        out_specs=in_vmem(1)[0],
+    velocity, density = pl.pallas_call(
+        krylov_kernel,
+        name="krylov",
+        out_shape=[jax.ShapeDtypeStruct((1, 120), f32)] * 2,
+        in_specs=in_vmem(4) + [pl.BlockSpec(memory_space=pl.ANY)],
+        out_specs=in_vmem(2),
         scratch_shapes=[
             pltpu.VMEM((24, 128), jnp.int32),
             pltpu.VMEM((8, TARGETS), f32),
             pltpu.VMEM((32, TARGETS), f32),
             pltpu.VMEM((32, TARGETS), bf16),
             pltpu.VMEM((SOURCES, 32), bf16),
-            pltpu.VMEM((SOURCES, 32), bf16),
-            pltpu.VMEM((16, SOURCES), bf16),
-            pltpu.VMEM((16, SOURCES), bf16),
-            pltpu.VMEM((16, TARGETS), f32),
-            pltpu.VMEM((16, TARGETS), f32),
-        ],
-    )(all_nodes, node_order.reshape(ROWS, 20, 128), fibers, forces)
-    velocity, density = pl.pallas_call(
-        krylov_kernel,
-        name="krylov",
-        out_shape=[jax.ShapeDtypeStruct((1, 120), f32)] * 2,
-        in_specs=in_vmem(1) + [pl.BlockSpec(memory_space=pl.ANY)],
-        out_specs=in_vmem(2),
-        scratch_shapes=[
+            pltpu.VMEM((48, SOURCES), bf16),
+            pltpu.VMEM((24, TARGETS), f32),
+            pltpu.VMEM((WIDTH // 128, 1, 128), f32),
             pltpu.VMEM((BLOCK, WIDTH), bf16),
             pltpu.VMEM((WIDTH // 128 + 1, 1, 128), f32),
             pltpu.VMEM((WIDTH // 128 + 1, 1, 128), f32),
@@ -572,7 +571,7 @@
             pltpu.SemaphoreType.DMA((2,)),
         ],
         compiler_params=pltpu.CompilerParams(collective_id=1, has_side_effects=True),
-    )(part, matrix_t)
+    )(all_nodes, node_order.reshape(ROWS, 20, 128), fibers, forces, matrix_t)
     return velocity.reshape(120), density.reshape(120)
 
 

time: 86.9 us -> 68 us (0.78)
  Pallas kernels: 81.8 us -> 63.4 us
    pallas_call x1 -> x0, Pallas kernels: 23.8 us -> none  [shards(): pl.pallas_call(stokes_kernel, name='stokes', out_shape=jax.ShapeDtypeStru...]
    pallas_call x1, Pallas kernels: 52 us -> 57.4 us  [shards(): pl.pallas_call(krylov_kernel, name='krylov', out_shape=[jax.ShapeDtypeStr...]
where the time goes in v2:
time: 68 us; the launch traced here: 67.7 us
  Pallas kernels  63.4 us (93%)
  local copies, waits for them, and re-layouts  3.66 us (5%)
    pallas_call x1, Pallas kernels, shards(): pl.pallas_call(krylov_kernel, name='krylov', out_shape=[jax.ShapeDtypeStr...  57.4 us
    pallas_call x1, Pallas kernels, shards(): pl.pallas_call(spread_nodes, name='spread_nodes', out_shape=jax.ShapeDtyp...  5.96 us
    unnamed x2, local copies, waits for them, and re-layouts  2.26 us
    reshape x1, local copies, waits for them, and re-layouts, shards(): node_order.reshape(ROWS, 20, 128)  1.4 us

profile of v2, /device:TPU:32, one launch (start us, length us, event | category | flops | bytes accessed | tf_op | source)
XLA Modules:
  0.0 67.7 jit_solution(13219687203134268334)
XLA Ops:
  0.6 1.4 %reshape.13.order_ref = s32[4,20,128]{2,1,0:T(8,128)} reshape(s32[10240]{0:T(1024)} %param.9) | data formatting | bytes 81920 | tf_op jit(solution)/shard_map/reshape | solution.py:574
  2.0 6.0 %spread_nodes.1.nodes_ref = f32[4,3,2560]{2,1,0:T(4,128)} custom-call(f32[3,2560]{1,0:T(4,128)} %nodes_ref.1), custom_call_target="tpu_custom_call" | custom-call | tf_op jit(solution)/shard_map/spread_nodes/pallas_call | solution.py:526
  8.0 57.4 %krylov.1 = (f32[1,120]{1,0:T(1,128)}, f32[1,120]{1,0:T(1,128)}) custom-call(f32[4,3,2560]{2,1,0:T(4,128)} %spread_nodes.1.nodes_ref, s32[4,20,128]{2,1,0:T(8,128)} %reshape.13.order_ref, f32[3,2048]{1,0:T(4,128)} %fibers_ref.1, f32[3,2048]{1,0:T(4,128)} %forces_ref.1, bf16[480,7680]{1,0:T(8,128)(2,1)} %matrix_ref.1), custom_call_target="tpu_custom_call" | custom-call | tf_op jit(solution)/shard_map/krylov/pallas_call | solution.py:539
  65.4 1.1 %copy.9 = f32[120]{0:T(128)} copy(f32[120]{0:T(128)} %bitcast.3) | data formatting | bytes 960
  66.6 1.1 %copy.10 = f32[120]{0:T(128)} copy(f32[120]{0:T(128)} %bitcast.2) | data formatting | bytes 960

commit v3 on v2

--- a/solution.py
+++ b/solution.py
@@ -1,4 +1,3 @@
-import functools
 import math
 
 import jax
@@ -38,50 +37,7 @@
     return found
 
 
-def spread_nodes(nodes_ref, all_ref, send_sem, recv_sem, own_sem):
-    row = lax.axis_index("row")
-    barrier = pltpu.get_barrier_semaphore()
-    for step in range(1, ROWS):
-        other = lax.rem(row + step, ROWS)
-        pl.semaphore_signal(
-            barrier, inc=1, device_id={"row": other}, device_id_type=MESH
-        )
-    own = pltpu.make_async_copy(nodes_ref, all_ref.at[row], own_sem)
-    own.start()
-    pl.semaphore_wait(barrier, ROWS - 1)
-    copies = []
-    for step in range(1, ROWS):
-        other = lax.rem(row + step, ROWS)
-        copy = pltpu.make_async_remote_copy(
-            src_ref=nodes_ref,
-            dst_ref=all_ref.at[row],
-            send_sem=send_sem.at[step],
-            recv_sem=recv_sem.at[step],
-            device_id={"row": other},
-            device_id_type=MESH,
-        )
-        copy.start()
-        copies.append(copy)
-    own.wait()
-    for copy in copies:
-        copy.wait()
-
-
-def velocity_part(
-    nodes_ref,
-    order_ref,
-    fibers_ref,
-    forces_ref,
-    out_ref,
-    index_ref,
-    target_ref,
-    feature_ref,
-    column_ref,
-    source_ref,
-    weight_ref,
-    sum_ref,
-):
-    row = lax.axis_index("row")
+def prepare_sources(fibers_ref, forces_ref, source_ref, weight_ref):
     fibers = fibers_ref[...]
     forces = forces_ref[...]
     place = [fibers[k : k + 1] for k in range(3)]
@@ -105,25 +61,38 @@
     one, two = pieces_of(moments, 2)
     weight_ref[...] = jnp.concatenate([one, two], axis=0).astype(bf16)
 
-    index_ref[pl.ds(0, 20), :] = order_ref[row]
+
+def indices(row, order_ref, index_ref):
+    index_ref[pl.ds(0, 20), :] = order_ref[pl.ds(row * 20, 20), :]
     index_ref[pl.ds(20, 4), :] = jnp.zeros((4, 128), jnp.int32)
     index = index_ref[...]
     high = index // 128
-    low = index - high * 128
-    found = tuple(jnp.zeros((24, 128), f32) for _ in range(3))
-
-    def pick(part, found):
-        found = list(found)
-        for tile in range(20):
-            hit = high == part * 20 + tile
-            for k in range(3):
-                line = nodes_ref[part, pl.ds(k, 1), pl.ds(tile * 128, 128)]
-                line = jnp.broadcast_to(line, (24, 128))
-                taken = jnp.take_along_axis(line, low, axis=1)
-                found[k] = jnp.where(hit, taken, found[k])
-        return tuple(found)
-
-    found = lax.fori_loop(0, ROWS, pick, found)
+    return high, index - high * 128
+
+
+def pick(part, nodes, high, low, found):
+    found = list(found)
+    for tile in range(20):
+        hit = high == part * 20 + tile
+        for k in range(3):
+            line = nodes[pl.ds(k, 1), pl.ds(tile * 128, 128)]
+            line = jnp.broadcast_to(line, (24, 128))
+            taken = jnp.take_along_axis(line, low, axis=1)
+            found[k] = jnp.where(hit, taken, found[k])
+    return found
+
+
+def velocity_part(
+    found,
+    between,
+    out_ref,
+    target_ref,
+    feature_ref,
+    column_ref,
+    source_ref,
+    weight_ref,
+    sum_ref,
+):
     square = found[0] * found[0] + found[1] * found[1] + found[2] * found[2]
     lines = []
     for k in range(3):
@@ -140,6 +109,7 @@
     column_ref[...] = feature_ref[...].astype(bf16)
 
     def across(turn, carry):
+        between(turn)
         at = pl.ds(pl.multiple_of(turn * WIDE, WIDE), WIDE)
         columns = column_ref[:, at]
         running = jnp.zeros((48, WIDE), f32)
@@ -189,8 +159,7 @@
     fibers_ref,
     forces_ref,
     matrix_ref,
-    velocity_ref,
-    density_ref,
+    result_ref,
     index_ref,
     target_ref,
     feature_ref,
@@ -198,6 +167,7 @@
     source_ref,
     weight_ref,
     sum_ref,
+    all_ref,
     part_ref,
     held,
     image_one,
@@ -217,6 +187,9 @@
     dot_recv,
     piece_send,
     piece_recv,
+    node_send,
+    node_recv,
+    round_sem,
 ):
     row = lax.axis_index("row")
     col = lax.axis_index("col")
@@ -231,32 +204,28 @@
     from_col = row * PLANE + col // 4
     self_in = level == row
 
+    mate = row + 1 - 2 * lax.rem(row, 2)
+    row_peers = [mate, lax.rem(row + 2, ROWS), lax.rem(mate + 2, ROWS)]
+    x_at = lax.rem(col // 4, 4)
+    z_at = lax.rem(col, 4)
+
+    def device(x, y, z):
+        return (row, y * PLANE + x * 4 + z)
+
+    x_line = [device(lax.rem(x_at + k, 4), level, z_at) for k in (1, 2, 3)]
+    y_line = [device(x_at, lax.rem(level + k, 4), z_at) for k in (1, 2, 3)]
+    z_near = [device(x_at, level, lax.rem(z_at + k, 4)) for k in (1, 3)]
+
     barrier = pltpu.get_barrier_semaphore()
-
-    def greet(step, carry):
-        other = lax.rem(col + step, COLS)
-
-        @pl.when(jnp.logical_not(jnp.logical_and(level == row, step == 0)))
-        def _():
+    near = [(peer, col) for peer in row_peers] + x_line + y_line + z_near
+    for peer in near:
+        pl.semaphore_signal(barrier, inc=1, device_id=peer, device_id_type=MESH)
+
+    def tell(which, peers):
+        for peer in peers:
             pl.semaphore_signal(
-                barrier, inc=1, device_id=(level, other), device_id_type=MESH
+                round_sem.at[which], inc=1, device_id=peer, device_id_type=MESH
             )
-
-        @pl.when(step > 0)
-        def _():
-            pl.semaphore_signal(
-                barrier, inc=1, device_id=(row, other), device_id_type=MESH
-            )
-
-        return carry
-
-    lax.fori_loop(0, COLS, greet, 0)
-
-    @pl.when(jnp.logical_not(piece_own))
-    def _():
-        pl.semaphore_signal(
-            barrier, inc=1, device_id=(from_row, from_col), device_id_type=MESH
-        )
 
     lane_node = lax.broadcasted_iota(jnp.int32, (256, 512), 0)
     lane_entry = lax.broadcasted_iota(jnp.int32, (256, 512), 1)
@@ -266,13 +235,42 @@
             jnp.logical_and(base == k, lane_entry < BLOCK), 1.0, 0.0
         ).astype(bf16)
 
+    prepare_sources(fibers_ref, forces_ref, source_ref, weight_ref)
+    high, low = indices(row, order_ref, index_ref)
+    pl.semaphore_wait(barrier, len(near))
+    node_copies = [
+        pltpu.make_async_remote_copy(
+            src_ref=nodes_ref,
+            dst_ref=all_ref.at[slot],
+            send_sem=node_send.at[slot],
+            recv_sem=node_recv.at[slot],
+            device_id=(peer, col),
+            device_id_type=MESH,
+        )
+        for slot, peer in enumerate(row_peers)
+    ]
+    for copy in node_copies:
+        copy.start()
+    tell(0, x_line)
+    found = pick(row, nodes_ref, high, low, [jnp.zeros((24, 128), f32)] * 3)
+    for slot, peer in enumerate(row_peers):
+        node_copies[slot].wait_recv()
+        found = pick(peer, all_ref.at[slot], high, low, found)
+
+    rounds = [x_line, y_line, z_near, z_near]
+
+    def between(turn):
+        for which in range(3):
+
+            @pl.when(turn == 2 * which + 1)
+            def _():
+                pl.semaphore_wait(round_sem.at[which], len(rounds[which]))
+                tell(which + 1, rounds[which + 1])
+
     velocity_part(
-        nodes_ref,
-        order_ref,
-        fibers_ref,
-        forces_ref,
+        found,
+        between,
         part_ref,
-        index_ref,
         target_ref,
         feature_ref,
         column_ref,
@@ -280,8 +278,7 @@
         weight_ref,
         sum_ref,
     )
-    peers = 2 * COLS - self_in.astype(jnp.int32) - piece_own.astype(jnp.int32)
-    pl.semaphore_wait(barrier, peers)
+    pl.semaphore_wait(round_sem.at[3], len(z_near))
 
     def send_blocks(stage, source, target, stride, scale, count):
         for z_step, x_step, row_step in FAR_FIRST:
@@ -486,7 +483,6 @@
     await_piece(1)
     velocity_piece = recv_piece[0]
     image_piece = recv_piece[1]
-    velocity_ref[...] = velocity_piece[:, :120]
     aa, ab, bb, al, bl, ll = await_dots(1, 6)
     entry_12 = ab + al
     entry_22 = bb + bl - entry_12 * ab
@@ -510,7 +506,10 @@
     result = weight_one * (velocity_piece * scale_one) + weight_two * (
         (image_piece - slide * velocity_piece) * scale_two
     )
-    density_ref[...] = result[:, :120]
+    result_ref[pl.ds(0, 1), :] = velocity_piece
+    result_ref[pl.ds(1, 1), :] = result
+    for copy in node_copies:
+        copy.wait_send()
     await_sent(0, recv_one)
     await_sent(1, recv_two)
     await_sent(2, recv_three)
@@ -523,25 +522,12 @@
 
 
 def shards(matrix_t, fibers, forces, nodes, node_order):
-    all_nodes = pl.pallas_call(
-        spread_nodes,
-        name="spread_nodes",
-        out_shape=jax.ShapeDtypeStruct((ROWS, 3, TARGETS), f32),
-        in_specs=in_vmem(1),
-        out_specs=in_vmem(1)[0],
-        scratch_shapes=[
-            pltpu.SemaphoreType.DMA((ROWS,)),
-            pltpu.SemaphoreType.DMA((ROWS,)),
-            pltpu.SemaphoreType.DMA,
-        ],
-        compiler_params=pltpu.CompilerParams(collective_id=0, has_side_effects=True),
-    )(nodes)
-    velocity, density = pl.pallas_call(
+    result = pl.pallas_call(
         krylov_kernel,
         name="krylov",
-        out_shape=[jax.ShapeDtypeStruct((1, 120), f32)] * 2,
+        out_shape=jax.ShapeDtypeStruct((2, 128), f32),
         in_specs=in_vmem(4) + [pl.BlockSpec(memory_space=pl.ANY)],
-        out_specs=in_vmem(2),
+        out_specs=in_vmem(1)[0],
         scratch_shapes=[
             pltpu.VMEM((24, 128), jnp.int32),
             pltpu.VMEM((8, TARGETS), f32),
@@ -550,6 +536,7 @@
             pltpu.VMEM((SOURCES, 32), bf16),
             pltpu.VMEM((48, SOURCES), bf16),
             pltpu.VMEM((24, TARGETS), f32),
+            pltpu.VMEM((3, 3, TARGETS), f32),
             pltpu.VMEM((WIDTH // 128, 1, 128), f32),
             pltpu.VMEM((BLOCK, WIDTH), bf16),
             pltpu.VMEM((WIDTH // 128 + 1, 1, 128), f32),
@@ -569,10 +556,13 @@
             pltpu.SemaphoreType.DMA((2,)),
             pltpu.SemaphoreType.DMA((2,)),
             pltpu.SemaphoreType.DMA((2,)),
+            pltpu.SemaphoreType.DMA((3,)),
+            pltpu.SemaphoreType.DMA((3,)),
+            pltpu.SemaphoreType.REGULAR((4,)),
         ],
-        compiler_params=pltpu.CompilerParams(collective_id=1, has_side_effects=True),
-    )(all_nodes, node_order.reshape(ROWS, 20, 128), fibers, forces, matrix_t)
-    return velocity.reshape(120), density.reshape(120)
+        compiler_params=pltpu.CompilerParams(collective_id=0, has_side_effects=True),
+    )(nodes, node_order.reshape(80, 128), fibers, forces, matrix_t)
+    return result[0, :120], result[1, :120]
 
 
 def solution(mesh):

time: 68 us -> 62 us (0.912)
  Pallas kernels: 63.4 us -> 59.9 us
  local copies, waits for them, and re-layouts: 3.66 us -> 1.25 us
    pallas_call x2 -> x1, Pallas kernels: 63.4 us -> 59.9 us  [shards(): pl.pallas_call(krylov_kernel, name='krylov', out_shape=jax.ShapeDtypeStru...]
    unnamed x2 -> x0, local copies, waits for them, and re-layouts: 2.26 us -> none
    reshape x1 -> x0, local copies, waits for them, and re-layouts: 1.4 us -> none  [shards(): node_order.reshape(ROWS, 20, 128)]
    squeeze x0 -> x1, local copies, waits for them, and re-layouts: none -> 1.25 us  [shards(): return (result[0, :120], result[1, :120])]
where the time goes in v3:
time: 62 us; the launch traced here: 61.8 us
  Pallas kernels  59.9 us (97%)
  local copies, waits for them, and re-layouts  1.25 us (2%)
  between operations  0.64 us (1%)
    pallas_call x1, Pallas kernels, shards(): pl.pallas_call(krylov_kernel, name='krylov', out_shape=jax.ShapeDtypeStru...  59.9 us
    squeeze x1, local copies, waits for them, and re-layouts, shards(): return (result[0, :120], result[1, :120])  1.25 us

profile of v3, /device:TPU:32, one launch (start us, length us, event | category | flops | bytes accessed | tf_op | source)
XLA Modules:
  0.0 61.8 jit_solution(5387730060287195973)
XLA Ops:
  0.6 59.9 %krylov.1 = f32[2,128]{1,0:T(2,128)} custom-call(f32[3,2560]{1,0:T(4,128)} %nodes_ref.1, s32[80,128]{1,0:T(8,128)} %bitcast.5, f32[3,2048]{1,0:T(4,128)} %fibers_ref.1, f32[3,2048]{1,0:T(4,128)} %forces_ref.1, bf16[480,7680]{1,0:T(8,128)(2,1)} %matrix_ref.1), custom_call_target="tpu_custom_call" | custom-call | tf_op jit(solution)/shard_map/krylov/pallas_call | solution.py:525
  60.6 1.3 %slice_bitcast_fusion = (f32[120]{0:T(128)}, f32[120]{0:T(128)}) fusion(f32[2,128]{1,0:T(2,128)} %krylov.1), kind=kLoop, calls=%fused_computation | loop fusion | bytes 1920 | tf_op jit(solution)/shard_map/squeeze | solution.py:565
